TPU v7x, 32 devices: a whole 2x2x4 slice. The times are simulated.
32 devices in a mesh: band: 4 (over x, core), lev: 8 (over z, y).
Axes of the slice: x: 2, y: 2, z: 4, core: 2. Of those that a mesh axis runs over, the one named last changes fastest.
Arguments:
- grid_in: bfloat16 [3, 32, 16, 2688], P(None, 'lev', 'band'), may hold values from -6 to 6
- row_shift: int32 [16], P('band'), may hold values from -3 to 0
- block_shift: int32 [16], P('band'), may hold values from 0 to 20
- interp_weights: bfloat16 [16, 4, 3, 128, 128], P('band'), may hold values from -0.15625 to 0.15625
- wave_order: int32 [128], replicated, may hold values from 0 to 127, as said below
- legendre: bfloat16 [128, 16, 1280], P('band'), may hold values from -1.5 to 1.5
Outputs:
- spectral: bfloat16 [3, 32, 128, 2, 1280], P(None, 'lev', 'band')
Inputs may be any that keep to these rules, and one draw needn't show every extreme that they name: `row_shift`: each latitude's stencil rows lie within 3 rows of it on both sides. `wave_order`: a permutation of the 128 wavenumbers; slots d * 32 to (d + 1) * 32 - 1 hold exactly one wavenumber of each aligned run of 4 consecutive wavenumbers.
All inputs are finite; a program needn't handle non-finite values.
Results may differ from a plain program's by a relative error of at most 0.0065.
Values may be sent and summed in bfloat16 or wider, within the bound.
A program may use at most 128 MiB of HBM per device.

v0:
```python
import math

import jax
import jax.numpy as jnp
from jax import lax
from jax.sharding import PartitionSpec as P

BLK = 128
HALO = 3
STENCIL = 4


def with_halo(block, sides, width):
    for axis, dim in sides:
        count = lax.axis_size(axis)
        forward = [(i, i + 1) for i in range(count - 1)]
        backward = [(target, source) for source, target in forward]
        low = lax.ppermute(
            lax.slice_in_dim(block, block.shape[dim] - width, None, axis=dim), axis, forward
        )
        high = lax.ppermute(lax.slice_in_dim(block, 0, width, axis=dim), axis, backward)
        block = jnp.concatenate([low, block, high], axis=dim)
    return block


def make_table(waves, longitudes):
    column = jnp.arange(longitudes, dtype=jnp.int32)[:, None]
    phase = column * waves[None, :] % longitudes
    angle = phase.astype(jnp.float32) * (2.0 * math.pi / longitudes)
    paired = jnp.stack([jnp.cos(angle), -jnp.sin(angle)], axis=2)
    return (paired.reshape(longitudes, 2 * waves.shape[0]) / math.sqrt(longitudes)).astype(
        jnp.bfloat16
    )


def stencil_rows(source, row_index, row_shift, block_shift):
    start = row_index + HALO + row_shift[row_index]
    rows = lax.dynamic_slice_in_dim(source, start, STENCIL, 2)
    rows = jnp.roll(rows, -block_shift[row_index] * BLK, axis=3)
    return rows.reshape(rows.shape[0], rows.shape[1], STENCIL, rows.shape[3] // BLK, BLK)


def vertical_terms(rows, weights, depth):
    total = None
    for level_step in range(3):
        term = jnp.einsum(
            "flsbj,sji->flbi",
            rows[:, level_step : level_step + depth],
            weights[:, level_step],
            preferred_element_type=jnp.float32,
        )
        total = term if total is None else total + term
    return total.reshape(total.shape[0], total.shape[1], total.shape[2] * total.shape[3])


def per_device(grid_in, row_shift, block_shift, interp_weights, wave_order, legendre):
    fields, depth, lat_rows, longitudes = grid_in.shape
    owned, latitudes, degrees = legendre.shape
    widened = with_halo(grid_in, (("band", 2),), HALO)
    extended = with_halo(widened, (("lev", 1),), 1)
    pieces = []
    for row_index in range(lat_rows):
        rows = stencil_rows(extended, row_index, row_shift, block_shift)
        pieces.append(vertical_terms(rows, interp_weights[row_index], depth))
    combined = jnp.stack(pieces, axis=2)
    interp = combined.astype(jnp.bfloat16)
    items = fields * depth
    own_waves = lax.dynamic_slice_in_dim(wave_order, lax.axis_index("band") * owned, owned)
    degree = jnp.arange(degrees, dtype=jnp.int32)[None, :]
    keep = degree >= own_waves[:, None]
    table = make_table(wave_order, longitudes)
    fourier = jnp.dot(
        interp.reshape(items * lat_rows, longitudes), table, preferred_element_type=jnp.float32
    )
    fourier = fourier.astype(jnp.bfloat16).reshape(items, lat_rows, table.shape[1])
    coeffs = lax.all_to_all(fourier, "band", split_axis=2, concat_axis=1, tiled=True)
    shaped = coeffs.reshape(coeffs.shape[0], latitudes, owned, 2)
    result = jnp.einsum("arqc,qrn->aqcn", shaped, legendre, preferred_element_type=jnp.float32)
    result = jnp.where(keep[None, :, None, :], result, jnp.zeros((), jnp.float32))
    spectral = result.astype(jnp.bfloat16)
    return spectral.reshape(fields, depth, owned, 2, degrees)


def solution(mesh):
    return jax.shard_map(
        per_device,
        mesh=mesh,
        in_specs=(
            P(None, "lev", "band", None),
            P("band"),
            P("band"),
            P("band", None, None, None, None),
            P(),
            P("band", None, None),
        ),
        out_specs=P(None, "lev", "band", None, None),
        check_vma=False,
    )
```

profile of v0, /device:TPU:9, one launch (start us, length us, event | category | flops | bytes accessed | tf_op | source)
XLA Modules:
  0.0 108.9 jit_solution(10730107957513051599)
XLA Ops:
  0.0 0.0 copy-start
  0.0 2.2 %fusion.27 = (bf16[3,4,3,2688]{3,2,1,0:T(4,128)(2,1)}, bf16[3,4,3,2688]{3,2,1,0:T(4,128)(2,1)}) fusion(bf16[3,4,4,2688]{3,2,1,0:T(4,128)(2,1)} %param.8), kind=kLoop, calls=%fused_computation.79 | loop fusion | bytes 774144 | tf_op jit(solution)/shard_map/slice | solution.py:19
  2.2 3.8 %collective-permute-start = (bf16[3,4,3,2688]{3,2,1,0:T(4,128)(2,1)}, bf16[3,4,3,2688]{3,2,1,0:T(4,128)(2,1)}, u32[]{:S(2)}, u32[]{:S(2)}) collective-permute-start(bf16[3,4,3,2688]{3,2,1,0:T(4,128)(2,1)} %get-tuple-element.16), channel_id=1, source_target_pairs={{0,8},{8,16},{16,24},{1,9},{9,17},{17,25},{2,10},{10,18},{18,26},{... | collective-permute-start | bytes 580616 | tf_op jit(solution)/shard_map/ppermute | solution.py:18
  6.0 1.9 %collective-permute-start.1 = (bf16[3,4,3,2688]{3,2,1,0:T(4,128)(2,1)}, bf16[3,4,3,2688]{3,2,1,0:T(4,128)(2,1)}, u32[]{:S(2)}, u32[]{:S(2)}) collective-permute-start(bf16[3,4,3,2688]{3,2,1,0:T(4,128)(2,1)} %get-tuple-element.17), channel_id=1, source_target_pairs={{8,0},{16,8},{24,16},{9,1},{17,9},{25,17},{10,2},{18,10},{26,18},{... | collective-permute-start | bytes 580616 | tf_op jit(solution)/shard_map/ppermute | solution.py:21
  7.9 1.5 %fusion.29 = (s32[1]{0:T(128)}, s32[1]{0:T(128)}, s32[1]{0:T(128)}, s32[1]{0:T(128)}) fusion(s32[4]{0:T(128)} %param.10), kind=kLoop, calls=%fused_computation.81 | loop fusion | bytes 32 | tf_op jit(solution)/shard_map/slice | solution.py:39
  12.1 7.3 %fusion.6 = (f32[2688,128,1]{1,0,2:T(8,128)S(1)}, f32[2688,128,1]{1,0,2:T(8,128)}) fusion(s32[128]{0:T(128)} %param.12), kind=kLoop, calls=%fused_computation.12 | loop fusion | flops 3440640 | bytes 2753024 | tf_op jit(solution)/shard_map/cos | solution.py:30
  19.4 0.1 dynamic_slice.18
  19.4 0.7 fusion.28
  25.4 0.0 copy-start.1
  25.4 2.5 %fusion.26 = (bf16[1,4,3,128,128]{4,3,2,1,0:T(8,128)(2,1)}, bf16[1,4,3,128,128]{4,3,2,1,0:T(8,128)(2,1)S(1)}, bf16[1,4,3,128,128]{4,3,2,1,0:T(8,128)(2,1)}, bf16[1,4,3,128,128]{4,3,2,1,0:T(8,128)(2,1)}) fusion(bf16[4,4,3,128,128]{4,3,2,1,0:T(8,128)(2,1)} %param.11), kind=kLoop, calls=%fused_computation.78 | loop fusion | bytes 3145728 | tf_op jit(solution)/shard_map/slice | solution.py:64
  27.9 1.4 %fusion.1 = bf16[2688,128,2]{1,0,2:T(8,128)(2,1)} fusion(f32[2688,128,1]{1,0,2:T(8,128)S(1)} %copy-done.1, f32[2688,128,1]{1,0,2:T(8,128)S(1)} %get-tuple-element.18), kind=kLoop, calls=%fused_computation.3 | loop fusion | flops 2064384 | bytes 4128768 | tf_op jit(solution)/shard_map/convert_element_type | solution.py:31
  29.3 4.8 %copy.57 = bf16[2688,128,2]{0,2,1:T(2,128)(2,1)} copy(bf16[2688,128,2]{1,0,2:T(8,128)(2,1)} %fusion.1) | data formatting | bytes 2752512 | tf_op jit(solution)/shard_map/convert_element_type | solution.py:31
  34.1 3.3 %convert_element_type.49 = bf16[2688,256]{0,1:T(8,128)(2,1)S(1)} reshape(bf16[2688,128,2]{0,2,1:T(2,128)(2,1)} %copy.57) | data formatting | bytes 2752512 | tf_op jit(solution)/shard_map/convert_element_type | solution.py:31
  37.5 2.1 %copy_bitcast_fusion.2 = (bf16[4,3,128,128]{3,2,0,1:T(8,128)(2,1)}, bf16[4,3,128,128]{3,2,0,1:T(8,128)(2,1)}) fusion(bf16[1,4,3,128,128]{4,3,2,1,0:T(8,128)(2,1)} %get-tuple-element.8, bf16[1,4,3,128,128]{4,3,2,1,0:T(8,128)(2,1)} %get-tuple-element.6), kind=kLoop, calls=%fused_computation.50 | loop fusion | bytes 1572864 | tf_op jit(solution)/shard_map/squeeze | solution.py:64
  39.6 0.0 collective-permute-done
  39.6 0.0 collective-permute-done.1
  39.6 0.0 copy-done.4
  39.6 1.2 %pad_maximum_fusion.3 = (bf16[3,1,10,2688]{3,2,1,0:T(8,128)(2,1)S(1)}, bf16[3,1,10,2688]{3,2,1,0:T(8,128)(2,1)S(1)}) fusion(bf16[3,4,3,2688]{3,2,1,0:T(4,128)(2,1)} %collective-permute-done.1, bf16[3,4,4,2688]{3,2,1,0:T(4,128)(2,1)S(1)} %copy-done.4, bf16[3,4,3,2688]{3,2,1,0:T(4,128)(2,1)} %collective-permute-done), kind=kLoop, calls=%fused_computation.59 | loop fusion | flops 967680 | bytes 967680 | tf_op jit(solution)/shard_map/slice | solution.py:19
  40.8 3.1 %collective-permute-start.2 = (bf16[3,1,10,2688]{3,2,1,0:T(8,128)(2,1)S(1)}, bf16[3,1,10,2688]{3,2,1,0:T(8,128)(2,1)S(1)}, u32[]{:S(2)}, u32[]{:S(2)}) collective-permute-start(bf16[3,1,10,2688]{3,2,1,0:T(8,128)(2,1)S(1)} %get-tuple-element.14), channel_id=1, source_target_pairs={{0,1},{1,2},{2,3},{3,4},{4,5},{5,6},{6,7},{8,9},{9,10},{10,11},{11... | collective-permute-start | bytes 483848 | tf_op jit(solution)/shard_map/ppermute | solution.py:18
  44.0 3.2 %collective-permute-start.3 = (bf16[3,1,10,2688]{3,2,1,0:T(8,128)(2,1)S(1)}, bf16[3,1,10,2688]{3,2,1,0:T(8,128)(2,1)S(1)}, u32[]{:S(2)}, u32[]{:S(2)}) collective-permute-start(bf16[3,1,10,2688]{3,2,1,0:T(8,128)(2,1)S(1)} %get-tuple-element.15), channel_id=1, source_target_pairs={{1,0},{2,1},{3,2},{4,3},{5,4},{6,5},{7,6},{9,8},{10,9},{11,10},{12... | collective-permute-start | bytes 483848 | tf_op jit(solution)/shard_map/ppermute | solution.py:21
  47.2 0.0 copy-done.5
  47.2 1.0 copy_bitcast_fusion
  48.2 6.6 %collective-permute-done.2 = bf16[3,1,10,2688]{3,2,1,0:T(8,128)(2,1)S(1)} collective-permute-done((bf16[3,1,10,2688]{3,2,1,0:T(8,128)(2,1)S(1)}, bf16[3,1,10,2688]{3,2,1,0:T(8,128)(2,1)S(1)}, u32[]{:S(2)}, u32[]{:S(2)}) %collective-permute-start.2) | collective-permute-done | bytes 161312 | tf_op jit(solution)/shard_map/ppermute | solution.py:18
  54.8 1.8 %collective-permute-done.3 = bf16[3,1,10,2688]{3,2,1,0:T(8,128)(2,1)S(1)} collective-permute-done((bf16[3,1,10,2688]{3,2,1,0:T(8,128)(2,1)S(1)}, bf16[3,1,10,2688]{3,2,1,0:T(8,128)(2,1)S(1)}, u32[]{:S(2)}, u32[]{:S(2)}) %collective-permute-start.3) | collective-permute-done | bytes 161312 | tf_op jit(solution)/shard_map/ppermute | solution.py:21
  56.6 1.7 %pad_maximum_fusion = bf16[3,6,10,2688]{3,2,1,0:T(8,128)(2,1)S(1)} fusion(bf16[3,1,10,2688]{3,2,1,0:T(8,128)(2,1)S(1)} %collective-permute-done.3, bf16[3,4,3,2688]{3,2,1,0:T(4,128)(2,1)} %collective-permute-done.1, bf16[3,4,4,2688]{3,2,1,0:T(4,128)(2,1)S(1)} %copy-done.4, bf16[3,4,3,2688]{3,2,1,0:T(4,128)(2,1)} %collective-permute-done, ...), kind=kLoop, calls=%fused_computation.5 | loop fusion | flops 4838400 | bytes 1935360 | tf_op jit(solution)/shard_map/concatenate | solution.py:22
  58.3 1.9 %constant_dynamic-slice_fusion.3 = (bf16[3,6,4,2688]{3,2,1,0:T(4,128)(2,1)S(1)}, bf16[3,6,4,2688]{3,2,1,0:T(4,128)(2,1)}, bf16[3,6,4,2688]{3,2,1,0:T(4,128)(2,1)}, bf16[3,6,4,2688]{3,2,1,0:T(4,128)(2,1)S(1)}) fusion(bf16[3,6,10,2688]{3,2,1,0:T(8,128)(2,1)S(1)} %pad_maximum_fusion, s32[]{:T(128)S(6)} %select_n.48, s32[]{:T(128)S(6)} %select_n.51, ...), kind=kLoop, calls=%fused_computation.77 | loop fusion | bytes 3096592 | tf_op jit(solution)/shard_map/dynamic_slice | solution.py:38
  60.2 2.4 %fusion.23 = (bf16[3,6,4,2688]{3,2,1,0:T(4,128)(2,1)}, bf16[3,6,4,2688]{3,2,1,0:T(4,128)(2,1)}) fusion(s32[]{:T(128)S(6)} %select_n.63, bf16[3,6,4,2688]{3,2,1,0:T(4,128)(2,1)S(1)} %get-tuple-element.13, s32[]{:T(128)S(6)} %select_n.61, bf16[3,6,4,2688]{3,2,1,0:T(4,128)(2,1)S(1)} %get-tuple-element.10), kind=kLoop, calls=%fused_computation.54 | loop fusion | flops 1548288 | bytes 1548296 | tf_op jit(solution)/shard_map/jit(_roll_dynamic)/concatenate | solution.py:39
  62.7 1.2 %reshape.167 = bf16[3,6,4,21,128]{4,3,2,1,0:T(8,128)(2,1)S(1)} reshape(bf16[3,6,4,2688]{3,2,1,0:T(4,128)(2,1)} %get-tuple-element.30) | data formatting | bytes 774144 | tf_op jit(solution)/shard_map/reshape | solution.py:40
  63.9 1.9 %convolution_bitcast_fusion.6 = f32[3,4,21,128]{3,2,1,0:T(8,128)} fusion(bf16[3,6,4,21,128]{4,3,2,1,0:T(8,128)(2,1)S(1)} %reshape.167, bf16[4,3,128,128]{3,2,0,1:T(8,128)(2,1)} %get-tuple-element.34), kind=kOutput, calls=%fused_computation.21 | convolution fusion | flops 33030144 | bytes 647168 | tf_op jit(solution)/shard_map/flsbj,sji->flbi/dot_general | solution.py:46
  65.8 1.8 %convolution_bitcast_fusion.7 = f32[3,4,21,128]{3,2,1,0:T(8,128)} fusion(bf16[3,6,4,21,128]{4,3,2,1,0:T(8,128)(2,1)S(1)} %reshape.167, bf16[4,3,128,128]{3,2,0,1:T(8,128)(2,1)} %get-tuple-element.34), kind=kOutput, calls=%fused_computation.22 | convolution fusion | flops 33030144 | bytes 647168 | tf_op jit(solution)/shard_map/flsbj,sji->flbi/dot_general | solution.py:46
  67.6 1.1 %reshape.166 = bf16[3,6,4,21,128]{4,3,2,1,0:T(8,128)(2,1)S(1)} reshape(bf16[3,6,4,2688]{3,2,1,0:T(4,128)(2,1)} %get-tuple-element.31) | data formatting | bytes 774144 | tf_op jit(solution)/shard_map/reshape | solution.py:40
  68.8 0.0 copy-start.7
  68.8 0.0 copy-start.8
  68.8 0.0 copy-done.6
  68.8 0.9 convolution_bitcast_fusion.9
  69.7 0.9 convolution_bitcast_fusion.10
  70.6 0.0 copy-done.7
  70.6 2.5 %fusion.21 = (bf16[3,6,4,2688]{3,2,1,0:T(4,128)(2,1)}, bf16[3,6,4,2688]{3,2,1,0:T(4,128)(2,1)}) fusion(s32[]{:T(128)S(6)} %select_n.67, bf16[3,6,4,2688]{3,2,1,0:T(4,128)(2,1)S(1)} %copy-done.7, s32[]{:T(128)S(6)} %select_n.65, bf16[3,6,4,2688]{3,2,1,0:T(4,128)(2,1)S(1)} %copy-done.8), kind=kLoop, calls=%fused_computation.52 | loop fusion | flops 1548288 | bytes 1548296 | tf_op jit(solution)/shard_map/jit(_roll_dynamic)/concatenate | solution.py:39
  73.1 1.9 %reshape.169 = bf16[3,6,4,21,128]{4,3,2,1,0:T(8,128)(2,1)} reshape(bf16[3,6,4,2688]{3,2,1,0:T(4,128)(2,1)} %get-tuple-element.28) | data formatting | bytes 774144 | tf_op jit(solution)/shard_map/reshape | solution.py:40
  75.0 1.9 %convolution_bitcast_fusion = f32[3,4,21,128]{3,2,1,0:T(8,128)} fusion(bf16[3,6,4,21,128]{4,3,2,1,0:T(8,128)(2,1)} %reshape.169, bf16[4,3,128,128]{3,2,0,1:T(8,128)(2,1)} %get-tuple-element.32), kind=kOutput, calls=%fused_computation.15 | convolution fusion | flops 33030144 | bytes 702464 | tf_op jit(solution)/shard_map/flsbj,sji->flbi/dot_general | solution.py:46
  76.8 1.9 %convolution_bitcast_fusion.1 = f32[3,4,21,128]{3,2,1,0:T(8,128)} fusion(bf16[3,6,4,21,128]{4,3,2,1,0:T(8,128)(2,1)} %reshape.169, bf16[4,3,128,128]{3,2,0,1:T(8,128)(2,1)} %get-tuple-element.32), kind=kOutput, calls=%fused_computation.16 | convolution fusion | flops 33030144 | bytes 702464 | tf_op jit(solution)/shard_map/flsbj,sji->flbi/dot_general | solution.py:46
  78.7 1.9 %reshape.168 = bf16[3,6,4,21,128]{4,3,2,1,0:T(8,128)(2,1)} reshape(bf16[3,6,4,2688]{3,2,1,0:T(4,128)(2,1)} %get-tuple-element.29) | data formatting | bytes 774144 | tf_op jit(solution)/shard_map/reshape | solution.py:40
  80.7 1.9 %convolution_bitcast_fusion.3 = f32[3,4,21,128]{3,2,1,0:T(8,128)} fusion(bf16[3,6,4,21,128]{4,3,2,1,0:T(8,128)(2,1)} %reshape.168, bf16[4,3,128,128]{3,2,0,1:T(8,128)(2,1)} %get-tuple-element.33), kind=kOutput, calls=%fused_computation.18 | convolution fusion | flops 33030144 | bytes 702464 | tf_op jit(solution)/shard_map/flsbj,sji->flbi/dot_general | solution.py:46
  82.6 1.9 %convolution_bitcast_fusion.4 = f32[3,4,21,128]{3,2,1,0:T(8,128)} fusion(bf16[3,6,4,21,128]{4,3,2,1,0:T(8,128)(2,1)} %reshape.168, bf16[4,3,128,128]{3,2,0,1:T(8,128)(2,1)} %get-tuple-element.33), kind=kOutput, calls=%fused_computation.19 | convolution fusion | flops 33030144 | bytes 702464 | tf_op jit(solution)/shard_map/flsbj,sji->flbi/dot_general | solution.py:46
  84.5 0.0 copy-done.3
  84.5 1.9 %fusion.19 = bf16[3,4,21,128]{3,2,1,0:T(8,128)(2,1)} fusion(f32[3,4,21,128]{3,2,1,0:T(8,128)} %convolution_bitcast_fusion.6, f32[3,4,21,128]{3,2,1,0:T(8,128)} %convolution_bitcast_fusion.7, bf16[3,6,4,21,128]{4,3,2,1,0:T(8,128)(2,1)S(1)} %copy-done.3, bf16[4,3,128,128]{3,2,0,1:T(8,128)(2,1)} %get-tuple-element.34), kind=kOutput, calls=%fused_computation.37 | convolution fusion | flops 33126912 | bytes 877568 | tf_op jit(solution)/shard_map/flsbj,sji->flbi/dot_general | solution.py:46
  86.4 1.6 %stack_reshape.17 = bf16[3,4,1,2688]{3,1,0,2:T(4,128)(2,1)} reshape(bf16[3,4,21,128]{3,2,1,0:T(8,128)(2,1)} %fusion.19) | data formatting | bytes 129024 | tf_op jit(solution)/shard_map/stack;reshape | solution.py:65
  88.0 1.9 %fusion.20 = bf16[3,4,21,128]{3,2,1,0:T(8,128)(2,1)} fusion(f32[3,4,21,128]{3,2,1,0:T(8,128)} %convolution_bitcast_fusion.9, f32[3,4,21,128]{3,2,1,0:T(8,128)} %convolution_bitcast_fusion.10, bf16[3,6,4,21,128]{4,3,2,1,0:T(8,128)(2,1)S(1)} %reshape.166, bf16[4,3,128,128]{3,2,0,1:T(8,128)(2,1)S(1)} %copy-done.6), kind=kOutput, calls=%fused_computation.38 | convolution fusion | flops 33126912 | bytes 896000 | tf_op jit(solution)/shard_map/flsbj,sji->flbi/dot_general | solution.py:46
  89.8 0.9 stack_reshape.16
  90.8 1.4 %fusion.17 = bf16[3,4,21,128]{3,2,1,0:T(8,128)(2,1)S(1)} fusion(f32[3,4,21,128]{3,2,1,0:T(8,128)} %convolution_bitcast_fusion, f32[3,4,21,128]{3,2,1,0:T(8,128)} %convolution_bitcast_fusion.1, bf16[3,6,4,21,128]{4,3,2,1,0:T(8,128)(2,1)} %reshape.169, bf16[4,3,128,128]{3,2,0,1:T(8,128)(2,1)} %get-tuple-element.32), kind=kOutput, calls=%fused_computation.35 | convolution fusion | flops 33126912 | bytes 932864 | tf_op jit(solution)/shard_map/flsbj,sji->flbi/dot_general | solution.py:46
  92.2 1.4 %fusion.18 = bf16[3,4,21,128]{3,2,1,0:T(8,128)(2,1)S(1)} fusion(f32[3,4,21,128]{3,2,1,0:T(8,128)} %convolution_bitcast_fusion.3, f32[3,4,21,128]{3,2,1,0:T(8,128)} %convolution_bitcast_fusion.4, bf16[3,6,4,21,128]{4,3,2,1,0:T(8,128)(2,1)} %reshape.168, bf16[4,3,128,128]{3,2,0,1:T(8,128)(2,1)} %get-tuple-element.33), kind=kOutput, calls=%fused_computation.36 | convolution fusion | flops 33126912 | bytes 932864 | tf_op jit(solution)/shard_map/flsbj,sji->flbi/dot_general | solution.py:46
  93.7 0.2 pad_maximum_fusion.4
  93.9 0.1 copy.56
  94.0 0.1 convert_element_type.46
  94.1 0.5 convolution_convert_fusion
  94.6 0.2 copy.58
  94.8 1.0 reshape.198
  95.9 3.6 %all-to-all-start = ((bf16[4,2,1536]{2,1,0:T(2,128)(2,1)}), bf16[4,2,1536]{2,1,0:T(2,128)(2,1)S(1)}, u32[]{:S(2)}, u32[]{:S(2)}) async-start(bf16[4,2,1536]{2,1,0:T(2,128)(2,1)} %reshape.198), calls=%async_computation | async-start | bytes 49152 | tf_op jit(solution)/shard_map/all_to_all | solution.py:76
  99.5 0.1 iota_compare_fusion
  99.6 3.1 %all-to-all-done = bf16[4,2,1536]{2,1,0:T(2,128)(2,1)S(1)} async-done(((bf16[4,2,1536]{2,1,0:T(2,128)(2,1)}), bf16[4,2,1536]{2,1,0:T(2,128)(2,1)S(1)}, u32[]{:S(2)}, u32[]{:S(2)}) %all-to-all-start) | async-done | bytes 24608 | tf_op jit(solution)/shard_map/all_to_all | solution.py:76
  102.7 0.6 reshape.199
  103.4 1.1 %fusion = bf16[12,32,2,1280]{3,0,2,1:T(8,128)(2,1)S(1)} fusion(pred[32,1280]{1,0:T(8,128)(4,1)S(1)} %iota_compare_fusion, bf16[32,16,1280]{2,1,0:T(8,128)(2,1)S(1)} %copy-done, bf16[12,16,32,2]{0,3,2,1:T(2,128)(2,1)S(1)} %bitcast.196), kind=kOutput, calls=%fused_computation.1 | convolution fusion | flops 33423360 | bytes 3342336 | tf_op jit(solution)/shard_map/arqc,qrn->aqcn/dot_general | solution.py:78
  104.5 1.1 copy.62
  105.6 3.3 %copy.63 = bf16[3,4,32,2,1280]{4,3,2,1,0:T(2,128)(2,1)} copy(bf16[3,4,32,2,1280]{4,2,3,1,0:T(8,128)(2,1)S(1)} %bitcast.195) | data formatting | bytes 3932160 | tf_op jit(solution)/shard_map/reshape | solution.py:81
  (19 shorter events, 0.2 us)
Async XLA Ops:
  0.0 103.4 %copy-start = (bf16[32,16,1280]{2,1,0:T(8,128)(2,1)S(1)}, bf16[32,16,1280]{2,1,0:T(8,128)(2,1)}, u32[]{:S(2)}) copy-start(bf16[32,16,1280]{2,1,0:T(8,128)(2,1)} %param.13) | copy-start | bytes 3932164
  2.2 17.2 %copy-start.11 = (s32[128]{0:T(128)S(1)}, s32[128]{0:T(128)}, u32[]{:S(2)}) copy-start(s32[128]{0:T(128)} %param.12) | copy-start | bytes 1540
  2.2 17.2 %copy-start.10 = (s32[4]{0:T(128)S(1)}, s32[4]{0:T(128)}, u32[]{:S(2)}) copy-start(s32[4]{0:T(128)} %param.9) | copy-start | bytes 52
  2.2 37.4 %collective-permute-start = (bf16[3,4,3,2688]{3,2,1,0:T(4,128)(2,1)}, bf16[3,4,3,2688]{3,2,1,0:T(4,128)(2,1)}, u32[]{:S(2)}, u32[]{:S(2)}) collective-permute-start(bf16[3,4,3,2688]{3,2,1,0:T(4,128)(2,1)} %get-tuple-element.16), channel_id=1, source_target_pairs={{0,8},{8,16},{16,24},{1,9},{9,17},{17,25},{2,10},{10,18},{18,26},{... | collective-permute-start | bytes 580616 | tf_op jit(solution)/shard_map/ppermute | solution.py:18
  6.0 33.6 %collective-permute-start.1 = (bf16[3,4,3,2688]{3,2,1,0:T(4,128)(2,1)}, bf16[3,4,3,2688]{3,2,1,0:T(4,128)(2,1)}, u32[]{:S(2)}, u32[]{:S(2)}) collective-permute-start(bf16[3,4,3,2688]{3,2,1,0:T(4,128)(2,1)} %get-tuple-element.17), channel_id=1, source_target_pairs={{8,0},{16,8},{24,16},{9,1},{17,9},{25,17},{10,2},{18,10},{26,18},{... | collective-permute-start | bytes 580616 | tf_op jit(solution)/shard_map/ppermute | solution.py:21
  25.4 2.5 %copy-start.1 = (f32[2688,128,1]{1,0,2:T(8,128)S(1)}, f32[2688,128,1]{1,0,2:T(8,128)}, u32[]{:S(2)}) copy-start(f32[2688,128,1]{1,0,2:T(8,128)} %get-tuple-element.19) | copy-start | bytes 4128772
  34.1 5.5 %copy-start.4 = (bf16[3,4,4,2688]{3,2,1,0:T(4,128)(2,1)S(1)}, bf16[3,4,4,2688]{3,2,1,0:T(4,128)(2,1)}, u32[]{:S(2)}) copy-start(bf16[3,4,4,2688]{3,2,1,0:T(4,128)(2,1)} %param.8) | copy-start | bytes 774148
  37.4 9.8 %copy-start.5 = (bf16[1,4,3,128,128]{4,3,2,1,0:T(8,128)(2,1)S(1)}, bf16[1,4,3,128,128]{4,3,2,1,0:T(8,128)(2,1)}, u32[]{:S(2)}) copy-start(bf16[1,4,3,128,128]{4,3,2,1,0:T(8,128)(2,1)} %get-tuple-element.9) | copy-start | bytes 1179652
  40.8 14.0 %collective-permute-start.2 = (bf16[3,1,10,2688]{3,2,1,0:T(8,128)(2,1)S(1)}, bf16[3,1,10,2688]{3,2,1,0:T(8,128)(2,1)S(1)}, u32[]{:S(2)}, u32[]{:S(2)}) collective-permute-start(bf16[3,1,10,2688]{3,2,1,0:T(8,128)(2,1)S(1)} %get-tuple-element.14), channel_id=1, source_target_pairs={{0,1},{1,2},{2,3},{3,4},{4,5},{5,6},{6,7},{8,9},{9,10},{10,11},{11... | collective-permute-start | bytes 483848 | tf_op jit(solution)/shard_map/ppermute | solution.py:18
  44.0 12.6 %collective-permute-start.3 = (bf16[3,1,10,2688]{3,2,1,0:T(8,128)(2,1)S(1)}, bf16[3,1,10,2688]{3,2,1,0:T(8,128)(2,1)S(1)}, u32[]{:S(2)}, u32[]{:S(2)}) collective-permute-start(bf16[3,1,10,2688]{3,2,1,0:T(8,128)(2,1)S(1)} %get-tuple-element.15), channel_id=1, source_target_pairs={{1,0},{2,1},{3,2},{4,3},{5,4},{6,5},{7,6},{9,8},{10,9},{11,10},{12... | collective-permute-start | bytes 483848 | tf_op jit(solution)/shard_map/ppermute | solution.py:21
  62.7 6.1 %copy-start.6 = (bf16[4,3,128,128]{3,2,0,1:T(8,128)(2,1)S(1)}, bf16[4,3,128,128]{3,2,0,1:T(8,128)(2,1)}, u32[]{:S(2)}) copy-start(bf16[4,3,128,128]{3,2,0,1:T(8,128)(2,1)} %get-tuple-element.35) | copy-start | bytes 1179652
  63.9 3.8 %copy-start.2 = (bf16[3,6,4,21,128]{4,3,2,1,0:T(8,128)(2,1)}, bf16[3,6,4,21,128]{4,3,2,1,0:T(8,128)(2,1)S(1)}, u32[]{:S(2)}) copy-start(bf16[3,6,4,21,128]{4,3,2,1,0:T(8,128)(2,1)S(1)} %reshape.167) | copy-start | bytes 1161220
  68.8 1.8 %copy-start.7 = (bf16[3,6,4,2688]{3,2,1,0:T(4,128)(2,1)S(1)}, bf16[3,6,4,2688]{3,2,1,0:T(4,128)(2,1)}, u32[]{:S(2)}) copy-start(bf16[3,6,4,2688]{3,2,1,0:T(4,128)(2,1)} %get-tuple-element.11) | copy-start | bytes 1161220
  68.8 1.8 %copy-start.8 = (bf16[3,6,4,2688]{3,2,1,0:T(4,128)(2,1)S(1)}, bf16[3,6,4,2688]{3,2,1,0:T(4,128)(2,1)}, u32[]{:S(2)}) copy-start(bf16[3,6,4,2688]{3,2,1,0:T(4,128)(2,1)} %get-tuple-element.12) | copy-start | bytes 1161220
  80.7 3.8 %copy-start.3 = (bf16[3,6,4,21,128]{4,3,2,1,0:T(8,128)(2,1)S(1)}, bf16[3,6,4,21,128]{4,3,2,1,0:T(8,128)(2,1)}, u32[]{:S(2)}) copy-start(bf16[3,6,4,21,128]{4,3,2,1,0:T(8,128)(2,1)} %copy-done.2) | copy-start | bytes 1161220
  89.8 3.8 %copy-start.9 = (bf16[3,4,1,2688]{3,1,0,2:T(4,128)(2,1)S(1)}, bf16[3,4,1,2688]{3,1,0,2:T(4,128)(2,1)}, u32[]{:S(2)}) copy-start(bf16[3,4,1,2688]{3,1,0,2:T(4,128)(2,1)} %stack_reshape.17) | copy-start | bytes 193540
  95.9 6.8 %all-to-all-start = ((bf16[4,2,1536]{2,1,0:T(2,128)(2,1)}), bf16[4,2,1536]{2,1,0:T(2,128)(2,1)S(1)}, u32[]{:S(2)}, u32[]{:S(2)}) async-start(bf16[4,2,1536]{2,1,0:T(2,128)(2,1)} %reshape.198), calls=%async_computation | async-start | bytes 49152 | tf_op jit(solution)/shard_map/all_to_all | solution.py:76
where the time goes:
time: 110 us; the launch traced here: 109 us
  local copies, waits for them, and re-layouts  35.3 us (32%)
  matrix products  21.3 us (19%)
  other arithmetic  16.8 us (15%)
  starting transfers between devices  15.7 us (14%)
  waiting for transfers between devices  11.5 us (10%)
  between operations  8.25 us (8%)
    dot_general x12, matrix products, vertical_terms(): jnp.einsum('flsbj,sji->flbi', rows[:, level_step:level_step + depth], wei...  19.7 us
    convert_element_type x2, local copies, waits for them, and re-layouts, make_table(): (paired.reshape(longitudes, 2 * waves.shape[0]) / math.sqrt(longitudes))....  8.07 us
    cos x1, other arithmetic, make_table(): paired = jnp.stack([jnp.cos(angle), -jnp.sin(angle)], axis=2)  7.3 us
    ppermute x2, starting transfers between devices, with_halo(): lax.ppermute(lax.slice_in_dim(block, block.shape[dim] - width, None, axis...  6.95 us
    ppermute x2, waiting for transfers between devices, with_halo(): lax.ppermute(lax.slice_in_dim(block, block.shape[dim] - width, None, axis...  6.57 us
    reshape x4, local copies, waits for them, and re-layouts, stencil_rows(): rows.reshape(rows.shape[0], rows.shape[1], STENCIL, rows.shape[3] // BLK,...  6.17 us
    ppermute x2, starting transfers between devices, with_halo(): lax.ppermute(lax.slice_in_dim(block, 0, width, axis=dim), axis, backward)  5.14 us
    concatenate x2, other arithmetic, stencil_rows(): rows = jnp.roll(rows, -block_shift[row_index] * BLK, axis=3)  4.86 us
  transfers between devices with their start and end apart: 5, of which 3 were waited for; matrix products, arithmetic and copies ran while one was open for 23% of the time, Pallas kernels for 0%

commit v1 on v0

v1 whole, which is shorter than its diff:
```python
import functools
import math

import jax
import jax.numpy as jnp
from jax import lax
from jax.experimental import pallas as pl
from jax.experimental.pallas import tpu as pltpu
from jax.sharding import PartitionSpec as P

BLK = 128
HALO = 3
STENCIL = 4
MESH = pl.DeviceIdType.MESH
DIRECTIONS = [(db, dl) for db in (-1, 0, 1) for dl in (-1, 0, 1) if (db, dl) != (0, 0)]


def round_up(value, multiple):
    return -(-value // multiple) * multiple


def spectral_kernel(
    bands, levs, fields, x_ref, w_ref, row_ref, block_ref, wave_ref, out_ref,
    ext, table, picks, shifted, outgoing, incoming, halo_send, halo_recv, all_send, all_recv,
):
    band, lev = lax.axis_index("band"), lax.axis_index("lev")
    lat_rows, depth, packed, _ = x_ref.shape
    waves = wave_ref.shape[1]
    owned = waves // bands
    items = fields * depth
    slots = shifted.shape[2]
    blocks = shifted.shape[1]
    longitudes = blocks * BLK

    def exists(db, dl):
        ok = None
        for here, step, count in ((band, db, bands), (lev, dl, levs)):
            if step == 0:
                continue
            one = here + 1 < count if step > 0 else here > 0
            ok = one if ok is None else jnp.logical_and(ok, one)
        return ok

    barrier = pltpu.get_barrier_semaphore()
    for k in range(1, bands):
        pl.semaphore_signal(
            barrier, inc=1, device_id={"band": lax.rem(band + k, bands), "lev": lev},
            device_id_type=MESH,
        )
    for db, dl in DIRECTIONS:
        if dl != 0:
            @pl.when(exists(db, dl))
            def _(db=db, dl=dl):
                pl.semaphore_signal(
                    barrier, inc=1, device_id={"band": band + db, "lev": lev + dl},
                    device_id_type=MESH,
                )

    source_rows = {1: (lat_rows - HALO, HALO), -1: (0, HALO), 0: (0, lat_rows)}
    target_rows = {1: (0, HALO), -1: (HALO + lat_rows, HALO), 0: (HALO, lat_rows)}
    source_levels = {1: (depth - 1, 1), -1: (0, 1), 0: (0, depth)}
    target_levels = {1: (0, 1), -1: (depth + 1, 1), 0: (1, depth)}

    near_bands = 1 + jnp.minimum(band, 1) + jnp.minimum(bands - 1 - band, 1)
    near_levs = jnp.minimum(lev, 1) + jnp.minimum(levs - 1 - lev, 1)
    pl.semaphore_wait(barrier, bands - 1 + near_bands * near_levs)

    def halo_copy(n, db, dl):
        return pltpu.make_async_remote_copy(
            src_ref=x_ref.at[pl.ds(*source_rows[db]), pl.ds(*source_levels[dl])],
            dst_ref=ext.at[pl.ds(*target_rows[db]), pl.ds(*target_levels[dl])],
            send_sem=halo_send.at[n],
            recv_sem=halo_recv.at[n],
            device_id={"band": band + db, "lev": lev + dl},
            device_id_type=MESH,
        )

    for n, (db, dl) in enumerate(DIRECTIONS):
        @pl.when(exists(db, dl))
        def _(n=n, db=db, dl=dl):
            halo_copy(n, db, dl).start()

    for n, (db, dl) in enumerate(DIRECTIONS):
        @pl.when(jnp.logical_not(exists(-db, -dl)))
        def _(db=db, dl=dl):
            rows, levels = target_rows[db], target_levels[dl]
            ext[pl.ds(*rows), pl.ds(*levels)] = jnp.zeros(
                (rows[1], levels[1], packed, BLK), ext.dtype
            )
    ext[pl.ds(HALO, lat_rows), pl.ds(1, depth)] = x_ref[...]

    wave = wave_ref[...]
    unit = 2.0 * math.pi / longitudes
    inner = lax.broadcasted_iota(jnp.int32, (BLK, waves), 0) * wave
    inner = lax.rem(inner, longitudes).astype(jnp.float32) * unit
    norm = 1.0 / math.sqrt(longitudes)
    inner_cos, inner_sin = jnp.cos(inner) * norm, jnp.sin(inner) * norm
    outer_rows = round_up(blocks, 8)
    outer = lax.broadcasted_iota(jnp.int32, (outer_rows, waves), 0) * wave
    outer = lax.rem(outer, blocks).astype(jnp.float32) * (unit * BLK)
    outer_cos, outer_sin = jnp.cos(outer), jnp.sin(outer)
    for b in range(blocks):
        ca, sa = outer_cos[b : b + 1], outer_sin[b : b + 1]
        table[b * BLK : (b + 1) * BLK, :waves] = (ca * inner_cos - sa * inner_sin).astype(
            table.dtype
        )
        table[b * BLK : (b + 1) * BLK, waves:] = (-(sa * inner_cos + ca * inner_sin)).astype(
            table.dtype
        )

    span = depth * packed
    item = lax.broadcasted_iota(jnp.int32, (slots, span), 0)
    field = jnp.zeros_like(item)
    for f in range(1, fields):
        field = field + (item >= f * depth).astype(jnp.int32)
    base = (item - field * depth) * packed + field * blocks
    base = lax.broadcasted_iota(jnp.int32, (slots, span), 1) - base
    base = jnp.where(item < items, base, -1)
    for r in range(lat_rows):
        for b in range(blocks):
            moved = block_ref[r] + b
            moved = jnp.where(moved >= blocks, moved - blocks, moved)
            picks[r, b * slots : (b + 1) * slots] = (
                jnp.where(base == moved, 1.0, 0.0).astype(picks.dtype)
            )

    for n, (db, dl) in enumerate(DIRECTIONS):
        @pl.when(exists(-db, -dl))
        def _(n=n, db=db, dl=dl):
            halo_copy(n, db, dl).wait_recv()

    for r in range(lat_rows):
        start = r + HALO + row_ref[r]
        rows = [ext[start + s].reshape((depth + 2) * packed, BLK) for s in range(STENCIL)]
        weights = [
            jnp.concatenate([w_ref[r, s, v] for v in range(3)], axis=1) for s in range(STENCIL)
        ]
        both = jnp.dot(
            jnp.concatenate(rows, axis=1), jnp.concatenate(weights, axis=0),
            preferred_element_type=jnp.float32,
        )
        total = (
            both[:span, :BLK]
            + both[packed : packed + span, BLK : 2 * BLK]
            + both[2 * packed : 2 * packed + span, 2 * BLK :]
        )
        chosen = jnp.dot(
            picks[r], total.astype(jnp.bfloat16), preferred_element_type=jnp.float32
        )
        shifted[r] = chosen.astype(shifted.dtype).reshape(blocks, slots, BLK)

    stacked = jnp.concatenate(
        [shifted[:, b].reshape(lat_rows * slots, BLK) for b in range(blocks)], axis=1
    )
    fourier = jnp.dot(stacked, table[...], preferred_element_type=jnp.float32)
    lane = lax.broadcasted_iota(jnp.int32, (lat_rows * slots, BLK), 1)
    for d in range(bands):
        group, offset = d * owned // BLK * BLK, d * owned % BLK
        real = fourier[:, group : group + BLK]
        imag = fourier[:, waves + group : waves + group + BLK]
        real = pltpu.roll(real, (BLK - offset) % BLK, 1)
        imag = pltpu.roll(imag, (BLK + owned - offset) % BLK, 1)
        outgoing[d] = jnp.where(lane < owned, real, imag).astype(outgoing.dtype)

    def all_copy(k):
        target = lax.rem(band + k, bands)
        return pltpu.make_async_remote_copy(
            src_ref=outgoing.at[target],
            dst_ref=incoming.at[band],
            send_sem=all_send.at[k],
            recv_sem=all_recv.at[k],
            device_id={"band": target, "lev": lev},
            device_id_type=MESH,
        )

    for k in range(1, bands):
        all_copy(k).start()
    out_ref[band] = outgoing[band]
    for n, (db, dl) in enumerate(DIRECTIONS):
        @pl.when(exists(db, dl))
        def _(n=n, db=db, dl=dl):
            halo_copy(n, db, dl).wait_send()
    for k in range(1, bands):
        all_copy(k).wait_recv()
        origin = lax.rem(band + bands - k, bands)
        out_ref[origin] = incoming[origin]
    for k in range(1, bands):
        all_copy(k).wait_send()


def per_device(bands, levs, grid_in, row_shift, block_shift, interp_weights, wave_order, legendre):
    fields, depth, lat_rows, longitudes = grid_in.shape
    owned, latitudes, degrees = legendre.shape
    waves = wave_order.shape[0]
    blocks = longitudes // BLK
    items = fields * depth
    packed = round_up(fields * blocks, 16)
    slots = round_up(items, 16)
    x = grid_in.reshape(fields, depth, lat_rows, blocks, BLK)
    x = jnp.transpose(x, (2, 1, 0, 3, 4)).reshape(lat_rows, depth, fields * blocks, BLK)
    x = jnp.pad(x, ((0, 0), (0, 0), (0, packed - fields * blocks), (0, 0)))
    vmem, smem = pl.BlockSpec(memory_space=pltpu.VMEM), pl.BlockSpec(memory_space=pltpu.SMEM)
    bf16 = jnp.bfloat16
    coeffs = pl.pallas_call(
        functools.partial(spectral_kernel, bands, levs, fields),
        out_shape=jax.ShapeDtypeStruct((bands, lat_rows * slots, BLK), bf16),
        in_specs=[vmem, vmem, smem, smem, vmem],
        out_specs=vmem,
        scratch_shapes=[
            pltpu.VMEM((lat_rows + 2 * HALO, depth + 2, packed, BLK), bf16),
            pltpu.VMEM((longitudes, 2 * waves), bf16),
            pltpu.VMEM((lat_rows, blocks * slots, depth * packed), bf16),
            pltpu.VMEM((lat_rows, blocks, slots, BLK), bf16),
            pltpu.VMEM((bands, lat_rows * slots, BLK), bf16),
            pltpu.VMEM((bands, lat_rows * slots, BLK), bf16),
            pltpu.SemaphoreType.DMA((len(DIRECTIONS),)),
            pltpu.SemaphoreType.DMA((len(DIRECTIONS),)),
            pltpu.SemaphoreType.DMA((bands,)),
            pltpu.SemaphoreType.DMA((bands,)),
        ],
        compiler_params=pltpu.CompilerParams(
            collective_id=0, has_side_effects=True, vmem_limit_bytes=48 << 20
        ),
    )(x, interp_weights, row_shift, block_shift, wave_order.reshape(1, waves))
    shaped = coeffs.reshape(bands * lat_rows, slots, BLK)[:, :items, : 2 * owned]
    shaped = shaped.reshape(latitudes, items, 2, owned)
    own_waves = lax.dynamic_slice_in_dim(wave_order, lax.axis_index("band") * owned, owned)
    degree = jnp.arange(degrees, dtype=jnp.int32)[None, :]
    keep = degree >= own_waves[:, None]
    result = jnp.einsum("racq,qrn->aqcn", shaped, legendre, preferred_element_type=jnp.float32)
    result = jnp.where(keep[None, :, None, :], result, jnp.zeros((), jnp.float32))
    return result.astype(bf16).reshape(fields, depth, owned, 2, degrees)


def solution(mesh):
    return jax.shard_map(
        functools.partial(per_device, mesh.shape["band"], mesh.shape["lev"]),
        mesh=mesh,
        in_specs=(
            P(None, "lev", "band", None),
            P("band"),
            P("band"),
            P("band", None, None, None, None),
            P(),
            P("band", None, None),
        ),
        out_specs=P(None, "lev", "band", None, None),
        check_vma=False,
    )
```

time: 110 us -> 24.3 us (0.22)
  local copies, waits for them, and re-layouts: 35.3 us -> 7.11 us
  matrix products: 21.3 us -> 0.81 us
  other arithmetic: 16.8 us -> 0.1 us
  Pallas kernels: 0 us -> 16 us
  starting transfers between devices: 15.7 us -> 0 us
  waiting for transfers between devices: 11.5 us -> 0 us
  between operations: 8.25 us -> 0.13 us
    dot_general x14 -> x1, matrix products: 21.3 us -> 0.81 us  [per_device(): jnp.einsum('racq,qrn->aqcn', shaped, legendre, preferred_element_type=jnp...]
    pallas_call x0 -> x1, Pallas kernels: none -> 16 us  [per_device(): pl.pallas_call(functools.partial(spectral_kernel, bands, levs, fields), o...]
    ppermute x4 -> x0, starting transfers between devices: 12.1 us -> none  [the longest x2 6.95 us: with_halo(): lax.ppermute(lax.slice_in_dim(block, block.shape[dim] - width, None, axis...]
    ppermute x4 -> x0, waiting for transfers between devices: 8.39 us -> none  [the longest x2 6.57 us: with_halo(): lax.ppermute(lax.slice_in_dim(block, block.shape[dim] - width, None, axis...]
    convert_element_type x4 -> x1, local copies, waits for them, and re-layouts: 9.22 us -> 1.08 us  [per_device(): return result.astype(bf16).reshape(fields, depth, owned, 2, degrees)]
    cos x1 -> x0, other arithmetic: 7.3 us -> none  [make_table(): paired = jnp.stack([jnp.cos(angle), -jnp.sin(angle)], axis=2)]
    slice x4 -> x0, local copies, waits for them, and re-layouts: 6.85 us -> none  [the longest x1 2.51 us: per_device(): pieces.append(vertical_terms(rows, interp_weights[row_index], depth))]
    concatenate x3 -> x0, other arithmetic: 6.59 us -> none  [the longest x2 4.86 us: stencil_rows(): rows = jnp.roll(rows, -block_shift[row_index] * BLK, axis=3)]
  transfers between devices with their start and end apart: 5 -> 0, of which waited for: 3 -> 0; matrix products, arithmetic and copies ran while one was open for 23% -> 0% of each run, Pallas kernels for 0% -> 0%
where the time goes in v1:
time: 24.3 us; the launch traced here: 24.1 us
  Pallas kernels  16 us (66%)
  local copies, waits for them, and re-layouts  7.11 us (29%)
  matrix products  0.81 us (3%)
    pallas_call x1, Pallas kernels, per_device(): pl.pallas_call(functools.partial(spectral_kernel, bands, levs, fields), o...  16 us
    reshape x1, local copies, waits for them, and re-layouts, per_device(): return result.astype(bf16).reshape(fields, depth, owned, 2, degrees)  3.29 us
    convert_element_type x1, local copies, waits for them, and re-layouts, per_device(): return result.astype(bf16).reshape(fields, depth, owned, 2, degrees)  1.08 us
    reshape x1, local copies, waits for them, and re-layouts, per_device(): x = grid_in.reshape(fields, depth, lat_rows, blocks, BLK)  1.05 us
    dynamic_slice x1, local copies, waits for them, and re-layouts, per_device(): lax.dynamic_slice_in_dim(wave_order, lax.axis_index('band') * owned, owned)  0.88 us
    dot_general x1, matrix products, per_device(): jnp.einsum('racq,qrn->aqcn', shaped, legendre, preferred_element_type=jnp...  0.81 us
    reshape x2, local copies, waits for them, and re-layouts, per_device(): shaped = shaped.reshape(latitudes, items, 2, owned)  0.56 us

profile of v1, /device:TPU:9, one launch (start us, length us, event | category | flops | bytes accessed | tf_op | source)
XLA Modules:
  0.0 24.1 jit_solution(8993831867174123699)
XLA Ops:
  0.0 0.0 copy-start
  0.0 0.0 copy-start.4
  0.0 0.0 copy-start.1
  0.0 0.0 copy-start.3
  0.0 0.0 copy-start.2
  0.0 0.9 %dynamic_slice.3 = s32[32]{0:T(128)S(1)} dynamic-slice(s32[128]{0:T(128)} %param.10, s32[]{:T(128)S(6)} %select_n.8), dynamic_slice_sizes={32} | dynamic-slice | bytes 260 | tf_op jit(solution)/shard_map/dynamic_slice | solution.py:227
  0.9 0.1 iota_compare_fusion
  1.0 1.1 %reshape.36 = bf16[3,4,4,21,128]{4,3,2,1,0:T(8,128)(2,1)S(1)} reshape(bf16[3,4,4,2688]{3,2,1,0:T(4,128)(2,1)} %param.6) | data formatting | bytes 516096 | tf_op jit(solution)/shard_map/reshape | solution.py:199
  2.1 0.1 copy.9
  2.3 0.0 copy-done.4
  2.3 0.0 copy-done.1
  2.3 0.0 copy-done.3
  2.3 0.0 copy-done.2
  2.4 16.0 %shard_map.64 = bf16[4,64,128]{2,1,0:T(8,128)(2,1)S(1)} custom-call(bf16[4,4,64,128]{3,2,1,0:T(8,128)(2,1)S(1)} %pad.4.x_ref, bf16[4,4,3,128,128]{4,3,2,1,0:T(8,128)(2,1)S(1)} %copy-done.1, s32[4]{0:T(128)S(1)} %copy-done.2, s32[4]{0:T(128)S(1)} %copy-done.3, s32[1,128]{1,0:T(1,128)S(1)} %bitcast.15), custom_call_target="tpu_custom_call" | custom-call | tf_op jit(solution)/shard_map/pallas_call | solution.py:204
  18.4 0.1 reshape.43
  18.5 0.5 %copy.12 = bf16[16,12,2,32]{0,1,2,3:T(8,128)(2,1)S(1)} copy(bf16[16,12,2,32]{3,2,1,0:T(2,128)(2,1)S(1)} %reshape.43) | data formatting | bytes 49152 | tf_op jit(solution)/shard_map/reshape | solution.py:226
  18.9 0.0 copy-done
  18.9 0.8 %fusion = bf16[12,32,2,1280]{3,0,2,1:T(8,128)(2,1)S(1)} fusion(bf16[16,12,2,32]{0,1,2,3:T(8,128)(2,1)S(1)} %copy.12, pred[32,1280]{1,0:T(8,128)(4,1)S(1)} %iota_compare_fusion, bf16[32,16,1280]{2,1,0:T(8,128)(2,1)S(1)} %copy-done), kind=kOutput, calls=%fused_computation.1 | convolution fusion | flops 33423360 | bytes 3342336 | tf_op jit(solution)/shard_map/racq,qrn->aqcn/dot_general | solution.py:230
  19.8 1.1 %copy.13 = bf16[12,32,2,1280]{3,1,2,0:T(8,128)(2,1)S(1)} copy(bf16[12,32,2,1280]{3,0,2,1:T(8,128)(2,1)S(1)} %fusion) | data formatting | bytes 3932160 | tf_op jit(solution)/shard_map/convert_element_type | solution.py:232
  20.8 3.3 %copy.14 = bf16[3,4,32,2,1280]{4,3,2,1,0:T(2,128)(2,1)} copy(bf16[3,4,32,2,1280]{4,2,3,1,0:T(8,128)(2,1)S(1)} %bitcast.16) | data formatting | bytes 3932160 | tf_op jit(solution)/shard_map/reshape | solution.py:232
  (2 shorter events, 0.1 us)
Async XLA Ops:
  0.0 18.9 %copy-start = (bf16[32,16,1280]{2,1,0:T(8,128)(2,1)S(1)}, bf16[32,16,1280]{2,1,0:T(8,128)(2,1)}, u32[]{:S(2)}) copy-start(bf16[32,16,1280]{2,1,0:T(8,128)(2,1)} %param.11) | copy-start | bytes 3932164
  0.0 2.3 %copy-start.4 = (s32[128]{0:T(128)S(1)}, s32[128]{0:T(128)}, u32[]{:S(2)}) copy-start(s32[128]{0:T(128)} %param.10) | copy-start | bytes 1540
  0.0 2.3 %copy-start.1 = (bf16[4,4,3,128,128]{4,3,2,1,0:T(8,128)(2,1)S(1)}, bf16[4,4,3,128,128]{4,3,2,1,0:T(8,128)(2,1)}, u32[]{:S(2)}) copy-start(bf16[4,4,3,128,128]{4,3,2,1,0:T(8,128)(2,1)} %w_ref.1) | copy-start | bytes 4718596
  0.0 2.3 %copy-start.3 = (s32[4]{0:T(128)S(1)}, s32[4]{0:T(128)}, u32[]{:S(2)}) copy-start(s32[4]{0:T(128)} %block_ref.1) | copy-start | bytes 52
  0.0 2.3 %copy-start.2 = (s32[4]{0:T(128)S(1)}, s32[4]{0:T(128)}, u32[]{:S(2)}) copy-start(s32[4]{0:T(128)} %row_ref.1) | copy-start | bytes 52

commit v2 on v1

--- a/solution.py
+++ b/solution.py
@@ -186,6 +186,94 @@
         out_ref[origin] = incoming[origin]
     for k in range(1, bands):
         all_copy(k).wait_send()
+
+
+def legendre_kernel(items, coeff_ref, legendre_ref, wave_ref, out_ref, spread, result, sems):
+    owned, latitudes, degrees = legendre_ref.shape
+    bands, rows, _ = coeff_ref.shape
+    slots = bands * rows // latitudes
+    group = BLK // latitudes
+    high = 2 * group
+    first = lax.axis_index("band") * owned
+
+    row = lax.broadcasted_iota(jnp.int32, (BLK, BLK), 0)
+    column = lax.broadcasted_iota(jnp.int32, (BLK, BLK), 1)
+    swap = row == lax.div(column, 2) + lax.rem(column, 2) * owned
+    swap = jnp.where(swap & (column < 2 * owned), 1.0, 0.0).astype(jnp.bfloat16)
+    coeffs = coeff_ref[...].reshape(bands * rows, BLK)
+    coeffs = jnp.dot(coeffs, swap, preferred_element_type=jnp.float32).astype(jnp.bfloat16)
+    lane = lax.broadcasted_iota(jnp.int32, (bands * rows, BLK), 1)
+    base = lax.broadcasted_iota(jnp.int32, (bands * rows, BLK), 0)
+    base = base - lax.rem(lane, latitudes) * slots
+    picks = [jnp.where(base == a, 1.0, 0.0).astype(jnp.bfloat16) for a in range(items)]
+    wide = lax.dot_general(
+        coeffs, jnp.concatenate(picks, axis=1), (((0,), (0,)), ((), ())),
+        preferred_element_type=jnp.float32,
+    )
+    spread[...] = wide[: 2 * owned].astype(spread.dtype)
+
+    row = lax.broadcasted_iota(jnp.int32, (high, BLK), 0)
+    column = lax.broadcasted_iota(jnp.int32, (high, BLK), 1)
+    diagonal = lax.div(row, 2) == lax.div(column, latitudes)
+    diagonal = jnp.where(diagonal, 1.0, 0.0).astype(jnp.bfloat16)
+    degree = lax.broadcasted_iota(jnp.int32, (latitudes, degrees), 1)
+    width = 2 * BLK if degrees % (2 * BLK) == 0 else BLK
+
+    def send(g):
+        part = pl.ds(g * group, group)
+        return pltpu.make_async_copy(result.at[:, part], out_ref.at[:, part], sems.at[g])
+
+    for g in range(owned // group):
+        left = jnp.concatenate(
+            [
+                spread[g * high : (g + 1) * high, a * BLK : (a + 1) * BLK] * diagonal
+                for a in range(items)
+            ],
+            axis=0,
+        )
+        right = []
+        for q in range(g * group, (g + 1) * group):
+            tile = legendre_ref[q]
+            right.append(jnp.where(degree >= wave_ref[first + q], tile, jnp.zeros_like(tile)))
+        right = jnp.concatenate(right, axis=0)
+        for n in range(0, degrees, width):
+            total = jnp.dot(left, right[:, n : n + width], preferred_element_type=jnp.float32)
+            result[:, g * group : (g + 1) * group, :, n : n + width] = total.astype(
+                result.dtype
+            ).reshape(items, group, 2, width)
+        send(g).start()
+    for g in range(owned // group):
+        send(g).wait()
+
+
+def legendre_tiled(coeffs, legendre, wave_order, items):
+    owned, latitudes, degrees = legendre.shape
+    shape = (items, owned, 2, degrees)
+    vmem, smem = pl.BlockSpec(memory_space=pltpu.VMEM), pl.BlockSpec(memory_space=pltpu.SMEM)
+    return pl.pallas_call(
+        functools.partial(legendre_kernel, items),
+        out_shape=jax.ShapeDtypeStruct(shape, jnp.bfloat16),
+        in_specs=[vmem, vmem, smem],
+        out_specs=pl.BlockSpec(memory_space=pltpu.HBM),
+        scratch_shapes=[
+            pltpu.VMEM((2 * owned, items * BLK), jnp.bfloat16),
+            pltpu.VMEM(shape, jnp.bfloat16),
+            pltpu.SemaphoreType.DMA((owned * latitudes // BLK,)),
+        ],
+        compiler_params=pltpu.CompilerParams(vmem_limit_bytes=16 << 20),
+    )(coeffs, legendre, wave_order)
+
+
+def legendre_einsum(coeffs, legendre, wave_order, items):
+    owned, latitudes, degrees = legendre.shape
+    shaped = coeffs.reshape(latitudes, -1, BLK)[:, :items, : 2 * owned]
+    shaped = shaped.reshape(latitudes, items, 2, owned)
+    own_waves = lax.dynamic_slice_in_dim(wave_order, lax.axis_index("band") * owned, owned)
+    degree = jnp.arange(degrees, dtype=jnp.int32)[None, :]
+    keep = degree >= own_waves[:, None]
+    result = jnp.einsum("racq,qrn->aqcn", shaped, legendre, preferred_element_type=jnp.float32)
+    result = jnp.where(keep[None, :, None, :], result, jnp.zeros((), jnp.float32))
+    return result.astype(jnp.bfloat16)
 
 
 def per_device(bands, levs, grid_in, row_shift, block_shift, interp_weights, wave_order, legendre):
@@ -222,14 +310,12 @@
             collective_id=0, has_side_effects=True, vmem_limit_bytes=48 << 20
         ),
     )(x, interp_weights, row_shift, block_shift, wave_order.reshape(1, waves))
-    shaped = coeffs.reshape(bands * lat_rows, slots, BLK)[:, :items, : 2 * owned]
-    shaped = shaped.reshape(latitudes, items, 2, owned)
-    own_waves = lax.dynamic_slice_in_dim(wave_order, lax.axis_index("band") * owned, owned)
-    degree = jnp.arange(degrees, dtype=jnp.int32)[None, :]
-    keep = degree >= own_waves[:, None]
-    result = jnp.einsum("racq,qrn->aqcn", shaped, legendre, preferred_element_type=jnp.float32)
-    result = jnp.where(keep[None, :, None, :], result, jnp.zeros((), jnp.float32))
-    return result.astype(bf16).reshape(fields, depth, owned, 2, degrees)
+    fits = latitudes % 16 == 0 and BLK % latitudes == 0
+    if fits and owned % (BLK // latitudes) == 0:
+        spectral = legendre_tiled(coeffs, legendre, wave_order, items)
+    else:
+        spectral = legendre_einsum(coeffs, legendre, wave_order, items)
+    return spectral.reshape(fields, depth, owned, 2, degrees)
 
 
 def solution(mesh):

time: 24.3 us -> 20.3 us (0.84)
  local copies, waits for them, and re-layouts: 7.11 us -> 1.5 us
  Pallas kernels: 16 us -> 18.6 us
  matrix products: 0.81 us -> 0 us
    reshape x3 -> x0, local copies, waits for them, and re-layouts: 3.85 us -> none  [the longest x1 3.29 us: per_device(): return result.astype(bf16).reshape(fields, depth, owned, 2, degrees)]
    pallas_call x0 -> x1, Pallas kernels: none -> 2.65 us  [legendre_tiled(): pl.pallas_call(functools.partial(legendre_kernel, items), out_shape=jax.S...]
    convert_element_type x1 -> x0, local copies, waits for them, and re-layouts: 1.08 us -> none  [per_device(): return result.astype(bf16).reshape(fields, depth, owned, 2, degrees)]
    dynamic_slice x1 -> x0, local copies, waits for them, and re-layouts: 0.88 us -> none  [per_device(): lax.dynamic_slice_in_dim(wave_order, lax.axis_index('band') * owned, owned)]
    dot_general x1 -> x0, matrix products: 0.81 us -> none  [per_device(): jnp.einsum('racq,qrn->aqcn', shaped, legendre, preferred_element_type=jnp...]
where the time goes in v2:
time: 20.3 us; the launch traced here: 20.2 us
  Pallas kernels  18.6 us (92%)
  local copies, waits for them, and re-layouts  1.5 us (7%)
    pallas_call x1, Pallas kernels, per_device(): pl.pallas_call(functools.partial(spectral_kernel, bands, levs, fields), o...  16 us
    pallas_call x1, Pallas kernels, legendre_tiled(): pl.pallas_call(functools.partial(legendre_kernel, items), out_shape=jax.S...  2.65 us
    reshape x1, local copies, waits for them, and re-layouts, per_device(): x = grid_in.reshape(fields, depth, lat_rows, blocks, BLK)  1.17 us

profile of v2, /device:TPU:9, one launch (start us, length us, event | category | flops | bytes accessed | tf_op | source)
XLA Modules:
  0.0 20.2 jit_solution(7955939661417940115)
XLA Ops:
  0.0 0.0 copy-start.2
  0.0 0.0 copy-start
  0.0 0.0 copy-start.4
  0.0 0.0 copy-start.3
  0.0 1.2 %reshape.12 = bf16[3,4,4,21,128]{4,3,2,1,0:T(8,128)(2,1)S(1)} reshape(bf16[3,4,4,2688]{3,2,1,0:T(4,128)(2,1)} %param.6) | data formatting | bytes 516096 | tf_op jit(solution)/shard_map/reshape | solution.py:287
  1.2 0.1 copy.8
  1.3 0.0 copy-start.1
  1.4 0.0 copy-done.2
  1.5 0.1 copy-done
  1.5 0.0 copy-done.4
  1.6 0.0 copy-done.3
  1.6 16.0 %shard_map.64.coeff_ref = bf16[4,64,128]{2,1,0:T(8,128)(2,1)S(1)} custom-call(bf16[4,4,64,128]{3,2,1,0:T(8,128)(2,1)S(1)} %pad.4.x_ref, bf16[4,4,3,128,128]{4,3,2,1,0:T(8,128)(2,1)S(1)} %copy-done, s32[4]{0:T(128)S(1)} %copy-done.3, s32[4]{0:T(128)S(1)} %copy-done.4, s32[1,128]{1,0:T(1,128)S(1)} %bitcast.4), custom_call_target="tpu_custom_call" | custom-call | tf_op jit(solution)/shard_map/pallas_call | solution.py:292
  17.5 0.0 copy-done.1
  17.5 2.6 %shard_map.65 = bf16[12,32,2,1280]{3,2,1,0:T(2,128)(2,1)} custom-call(bf16[4,64,128]{2,1,0:T(8,128)(2,1)S(1)} %shard_map.64.coeff_ref, bf16[32,16,1280]{2,1,0:T(8,128)(2,1)S(1)} %copy-done.1, s32[128]{0:T(128)S(1)} %copy-done.2), custom_call_target="tpu_custom_call" | custom-call | tf_op jit(solution)/shard_map/pallas_call | solution.py:253
  (2 shorter events, 0.1 us)
Async XLA Ops:
  0.0 1.4 %copy-start.2 = (s32[128]{0:T(128)S(1)}, s32[128]{0:T(128)}, u32[]{:S(2)}) copy-start(s32[128]{0:T(128)} %wave_ref.1) | copy-start | bytes 1540
  0.0 1.5 %copy-start = (bf16[4,4,3,128,128]{4,3,2,1,0:T(8,128)(2,1)S(1)}, bf16[4,4,3,128,128]{4,3,2,1,0:T(8,128)(2,1)}, u32[]{:S(2)}) copy-start(bf16[4,4,3,128,128]{4,3,2,1,0:T(8,128)(2,1)} %w_ref.1) | copy-start | bytes 4718596
  0.0 1.5 %copy-start.4 = (s32[4]{0:T(128)S(1)}, s32[4]{0:T(128)}, u32[]{:S(2)}) copy-start(s32[4]{0:T(128)} %block_ref.1) | copy-start | bytes 52
  0.0 1.5 %copy-start.3 = (s32[4]{0:T(128)S(1)}, s32[4]{0:T(128)}, u32[]{:S(2)}) copy-start(s32[4]{0:T(128)} %row_ref.1) | copy-start | bytes 52
  1.3 16.2 %copy-start.1 = (bf16[32,16,1280]{2,1,0:T(8,128)(2,1)S(1)}, bf16[32,16,1280]{2,1,0:T(8,128)(2,1)}, u32[]{:S(2)}) copy-start(bf16[32,16,1280]{2,1,0:T(8,128)(2,1)} %legendre_ref.1) | copy-start | bytes 3932164

commit v3 on v2

--- a/solution.py
+++ b/solution.py
@@ -12,7 +12,7 @@
 HALO = 3
 STENCIL = 4
 MESH = pl.DeviceIdType.MESH
-DIRECTIONS = [(db, dl) for db in (-1, 0, 1) for dl in (-1, 0, 1) if (db, dl) != (0, 0)]
+SIDES = (1, -1)
 
 
 def round_up(value, multiple):
@@ -21,7 +21,8 @@
 
 def spectral_kernel(
     bands, levs, fields, x_ref, w_ref, row_ref, block_ref, wave_ref, out_ref,
-    ext, table, picks, shifted, outgoing, incoming, halo_send, halo_recv, all_send, all_recv,
+    ext, edges, table, picks, sums, shifted, outgoing, incoming,
+    lev_send, lev_recv, band_send, band_recv, corner_send, corner_recv, all_send, all_recv,
 ):
     band, lev = lax.axis_index("band"), lax.axis_index("lev")
     lat_rows, depth, packed, _ = x_ref.shape
@@ -32,62 +33,77 @@
     blocks = shifted.shape[1]
     longitudes = blocks * BLK
 
-    def exists(db, dl):
-        ok = None
-        for here, step, count in ((band, db, bands), (lev, dl, levs)):
-            if step == 0:
-                continue
-            one = here + 1 < count if step > 0 else here > 0
-            ok = one if ok is None else jnp.logical_and(ok, one)
-        return ok
+    def has(here, step, count):
+        return here + 1 < count if step > 0 else here > 0
 
     barrier = pltpu.get_barrier_semaphore()
+    for step in SIDES:
+        @pl.when(has(lev, step, levs))
+        def _(step=step):
+            pl.semaphore_signal(
+                barrier, inc=1, device_id={"band": band, "lev": lev + step}, device_id_type=MESH
+            )
     for k in range(1, bands):
         pl.semaphore_signal(
             barrier, inc=1, device_id={"band": lax.rem(band + k, bands), "lev": lev},
             device_id_type=MESH,
         )
-    for db, dl in DIRECTIONS:
-        if dl != 0:
-            @pl.when(exists(db, dl))
-            def _(db=db, dl=dl):
-                pl.semaphore_signal(
-                    barrier, inc=1, device_id={"band": band + db, "lev": lev + dl},
-                    device_id_type=MESH,
-                )
-
-    source_rows = {1: (lat_rows - HALO, HALO), -1: (0, HALO), 0: (0, lat_rows)}
-    target_rows = {1: (0, HALO), -1: (HALO + lat_rows, HALO), 0: (HALO, lat_rows)}
-    source_levels = {1: (depth - 1, 1), -1: (0, 1), 0: (0, depth)}
-    target_levels = {1: (0, 1), -1: (depth + 1, 1), 0: (1, depth)}
-
-    near_bands = 1 + jnp.minimum(band, 1) + jnp.minimum(bands - 1 - band, 1)
+
+    first_row = {1: lat_rows - HALO, -1: 0}
+    landing = {1: 0, -1: HALO + lat_rows}
+
+    def lev_copy(n, step):
+        return pltpu.make_async_remote_copy(
+            src_ref=x_ref.at[:, depth - 1 if step > 0 else 0],
+            dst_ref=edges.at[n, pl.ds(HALO, lat_rows)],
+            send_sem=lev_send.at[n],
+            recv_sem=lev_recv.at[n],
+            device_id={"band": band, "lev": lev + step},
+            device_id_type=MESH,
+        )
+
+    def band_copy(n, step):
+        return pltpu.make_async_remote_copy(
+            src_ref=x_ref.at[pl.ds(first_row[step], HALO)],
+            dst_ref=ext.at[pl.ds(landing[step], HALO)],
+            send_sem=band_send.at[n],
+            recv_sem=band_recv.at[n],
+            device_id={"band": band + step, "lev": lev},
+            device_id_type=MESH,
+        )
+
+    def corner_copy(n, m, step):
+        return pltpu.make_async_remote_copy(
+            src_ref=edges.at[n, pl.ds(HALO + first_row[step], HALO)],
+            dst_ref=edges.at[n, pl.ds(landing[step], HALO)],
+            send_sem=corner_send.at[n, m],
+            recv_sem=corner_recv.at[n, m],
+            device_id={"band": band + step, "lev": lev},
+            device_id_type=MESH,
+        )
+
     near_levs = jnp.minimum(lev, 1) + jnp.minimum(levs - 1 - lev, 1)
-    pl.semaphore_wait(barrier, bands - 1 + near_bands * near_levs)
-
-    def halo_copy(n, db, dl):
-        return pltpu.make_async_remote_copy(
-            src_ref=x_ref.at[pl.ds(*source_rows[db]), pl.ds(*source_levels[dl])],
-            dst_ref=ext.at[pl.ds(*target_rows[db]), pl.ds(*target_levels[dl])],
-            send_sem=halo_send.at[n],
-            recv_sem=halo_recv.at[n],
-            device_id={"band": band + db, "lev": lev + dl},
-            device_id_type=MESH,
-        )
-
-    for n, (db, dl) in enumerate(DIRECTIONS):
-        @pl.when(exists(db, dl))
-        def _(n=n, db=db, dl=dl):
-            halo_copy(n, db, dl).start()
-
-    for n, (db, dl) in enumerate(DIRECTIONS):
-        @pl.when(jnp.logical_not(exists(-db, -dl)))
-        def _(db=db, dl=dl):
-            rows, levels = target_rows[db], target_levels[dl]
-            ext[pl.ds(*rows), pl.ds(*levels)] = jnp.zeros(
-                (rows[1], levels[1], packed, BLK), ext.dtype
-            )
-    ext[pl.ds(HALO, lat_rows), pl.ds(1, depth)] = x_ref[...]
+    pl.semaphore_wait(barrier, bands - 1 + near_levs)
+    for n, step in enumerate(SIDES):
+        @pl.when(has(lev, step, levs))
+        def _(n=n, step=step):
+            lev_copy(n, step).start()
+    for n, step in enumerate(SIDES):
+        @pl.when(has(band, step, bands))
+        def _(n=n, step=step):
+            band_copy(n, step).start()
+
+    for n, step in enumerate(SIDES):
+        @pl.when(jnp.logical_not(has(band, -step, bands)))
+        def _(step=step):
+            ext[pl.ds(landing[step], HALO)] = jnp.zeros((HALO, depth, packed, BLK), ext.dtype)
+            for m in range(2):
+                edges[m, pl.ds(landing[step], HALO)] = jnp.zeros((HALO, packed, BLK), ext.dtype)
+
+        @pl.when(jnp.logical_not(has(lev, -step, levs)))
+        def _(n=n):
+            edges[n] = jnp.zeros(edges.shape[1:], edges.dtype)
+    ext[pl.ds(HALO, lat_rows)] = x_ref[...]
 
     wave = wave_ref[...]
     unit = 2.0 * math.pi / longitudes
@@ -124,14 +140,25 @@
                 jnp.where(base == moved, 1.0, 0.0).astype(picks.dtype)
             )
 
-    for n, (db, dl) in enumerate(DIRECTIONS):
-        @pl.when(exists(-db, -dl))
-        def _(n=n, db=db, dl=dl):
-            halo_copy(n, db, dl).wait_recv()
+    for n, step in enumerate(SIDES):
+        @pl.when(has(lev, -step, levs))
+        def _(n=n, step=step):
+            lev_copy(n, step).wait_recv()
+            for m, side in enumerate(SIDES):
+                @pl.when(has(band, side, bands))
+                def _():
+                    corner_copy(n, m, side).start()
+    for n, step in enumerate(SIDES):
+        @pl.when(has(band, -step, bands))
+        def _(n=n, step=step):
+            band_copy(n, step).wait_recv()
+
+    def level(array, l, v):
+        return array[l * packed : (l + 1) * packed, v * BLK : (v + 1) * BLK]
 
     for r in range(lat_rows):
         start = r + HALO + row_ref[r]
-        rows = [ext[start + s].reshape((depth + 2) * packed, BLK) for s in range(STENCIL)]
+        rows = [ext[start + s].reshape(span, BLK) for s in range(STENCIL)]
         weights = [
             jnp.concatenate([w_ref[r, s, v] for v in range(3)], axis=1) for s in range(STENCIL)
         ]
@@ -139,14 +166,31 @@
             jnp.concatenate(rows, axis=1), jnp.concatenate(weights, axis=0),
             preferred_element_type=jnp.float32,
         )
-        total = (
-            both[:span, :BLK]
-            + both[packed : packed + span, BLK : 2 * BLK]
-            + both[2 * packed : 2 * packed + span, 2 * BLK :]
-        )
-        chosen = jnp.dot(
-            picks[r], total.astype(jnp.bfloat16), preferred_element_type=jnp.float32
-        )
+        for l in range(depth):
+            total = level(both, l, 1)
+            if l > 0:
+                total = total + level(both, l - 1, 0)
+            if l < depth - 1:
+                total = total + level(both, l + 1, 2)
+            sums[r, l] = total
+
+    for n, step in enumerate(SIDES):
+        for m, side in enumerate(SIDES):
+            @pl.when(jnp.logical_and(has(lev, -step, levs), has(band, -side, bands)))
+            def _(n=n, m=m, side=side):
+                corner_copy(n, m, side).wait_recv()
+
+    for r in range(lat_rows):
+        start = r + HALO + row_ref[r]
+        for n, v, l in ((0, 0, 0), (1, 2, depth - 1)):
+            rows = [edges[n, start + s] for s in range(STENCIL)]
+            weights = [w_ref[r, s, v] for s in range(STENCIL)]
+            sums[r, l] += jnp.dot(
+                jnp.concatenate(rows, axis=1), jnp.concatenate(weights, axis=0),
+                preferred_element_type=jnp.float32,
+            )
+        total = sums[r].reshape(span, BLK).astype(jnp.bfloat16)
+        chosen = jnp.dot(picks[r], total, preferred_element_type=jnp.float32)
         shifted[r] = chosen.astype(shifted.dtype).reshape(blocks, slots, BLK)
 
     stacked = jnp.concatenate(
@@ -176,10 +220,18 @@
     for k in range(1, bands):
         all_copy(k).start()
     out_ref[band] = outgoing[band]
-    for n, (db, dl) in enumerate(DIRECTIONS):
-        @pl.when(exists(db, dl))
-        def _(n=n, db=db, dl=dl):
-            halo_copy(n, db, dl).wait_send()
+    for n, step in enumerate(SIDES):
+        @pl.when(has(lev, step, levs))
+        def _(n=n, step=step):
+            lev_copy(n, step).wait_send()
+
+        @pl.when(has(band, step, bands))
+        def _(n=n, step=step):
+            band_copy(n, step).wait_send()
+            for m in range(2):
+                @pl.when(has(lev, -SIDES[m], levs))
+                def _():
+                    corner_copy(m, n, step).wait_send()
     for k in range(1, bands):
         all_copy(k).wait_recv()
         origin = lax.rem(band + bands - k, bands)
@@ -295,14 +347,20 @@
         in_specs=[vmem, vmem, smem, smem, vmem],
         out_specs=vmem,
         scratch_shapes=[
-            pltpu.VMEM((lat_rows + 2 * HALO, depth + 2, packed, BLK), bf16),
+            pltpu.VMEM((lat_rows + 2 * HALO, depth, packed, BLK), bf16),
+            pltpu.VMEM((2, lat_rows + 2 * HALO, packed, BLK), bf16),
             pltpu.VMEM((longitudes, 2 * waves), bf16),
             pltpu.VMEM((lat_rows, blocks * slots, depth * packed), bf16),
+            pltpu.VMEM((lat_rows, depth, packed, BLK), jnp.float32),
             pltpu.VMEM((lat_rows, blocks, slots, BLK), bf16),
             pltpu.VMEM((bands, lat_rows * slots, BLK), bf16),
             pltpu.VMEM((bands, lat_rows * slots, BLK), bf16),
-            pltpu.SemaphoreType.DMA((len(DIRECTIONS),)),
-            pltpu.SemaphoreType.DMA((len(DIRECTIONS),)),
+            pltpu.SemaphoreType.DMA((2,)),
+            pltpu.SemaphoreType.DMA((2,)),
+            pltpu.SemaphoreType.DMA((2,)),
+            pltpu.SemaphoreType.DMA((2,)),
+            pltpu.SemaphoreType.DMA((2, 2)),
+            pltpu.SemaphoreType.DMA((2, 2)),
             pltpu.SemaphoreType.DMA((bands,)),
             pltpu.SemaphoreType.DMA((bands,)),
         ],

time: 20.3 us -> 18.6 us (0.916)
  Pallas kernels: 18.6 us -> 16.9 us
    pallas_call x1, Pallas kernels: 16 us -> 14.3 us  [per_device(): pl.pallas_call(functools.partial(spectral_kernel, bands, levs, fields), o...]
where the time goes in v3:
time: 18.6 us; the launch traced here: 18.5 us
  Pallas kernels  16.9 us (91%)
  local copies, waits for them, and re-layouts  1.5 us (8%)
    pallas_call x1, Pallas kernels, per_device(): pl.pallas_call(functools.partial(spectral_kernel, bands, levs, fields), o...  14.3 us
    pallas_call x1, Pallas kernels, legendre_tiled(): pl.pallas_call(functools.partial(legendre_kernel, items), out_shape=jax.S...  2.65 us
    reshape x1, local copies, waits for them, and re-layouts, per_device(): x = grid_in.reshape(fields, depth, lat_rows, blocks, BLK)  1.17 us

profile of v3, /device:TPU:9, one launch (start us, length us, event | category | flops | bytes accessed | tf_op | source)
XLA Modules:
  0.0 18.5 jit_solution(9369609720936222075)
XLA Ops:
  0.0 0.0 copy-start.2
  0.0 0.0 copy-start
  0.0 0.0 copy-start.4
  0.0 0.0 copy-start.3
  0.0 1.2 %reshape.12 = bf16[3,4,4,21,128]{4,3,2,1,0:T(8,128)(2,1)S(1)} reshape(bf16[3,4,4,2688]{3,2,1,0:T(4,128)(2,1)} %param.6) | data formatting | bytes 516096 | tf_op jit(solution)/shard_map/reshape | solution.py:339
  1.2 0.1 copy.8
  1.3 0.0 copy-start.1
  1.4 0.0 copy-done.2
  1.5 0.1 copy-done
  1.5 0.0 copy-done.4
  1.6 0.0 copy-done.3
  1.6 14.3 %shard_map.64.coeff_ref = bf16[4,64,128]{2,1,0:T(8,128)(2,1)S(1)} custom-call(bf16[4,4,64,128]{3,2,1,0:T(8,128)(2,1)S(1)} %pad.4.x_ref, bf16[4,4,3,128,128]{4,3,2,1,0:T(8,128)(2,1)S(1)} %copy-done, s32[4]{0:T(128)S(1)} %copy-done.3, s32[4]{0:T(128)S(1)} %copy-done.4, s32[1,128]{1,0:T(1,128)S(1)} %bitcast.4), custom_call_target="tpu_custom_call" | custom-call | tf_op jit(solution)/shard_map/pallas_call | solution.py:344
  15.8 0.0 copy-done.1
  15.8 2.7 %shard_map.65 = bf16[12,32,2,1280]{3,2,1,0:T(2,128)(2,1)} custom-call(bf16[4,64,128]{2,1,0:T(8,128)(2,1)S(1)} %shard_map.64.coeff_ref, bf16[32,16,1280]{2,1,0:T(8,128)(2,1)S(1)} %copy-done.1, s32[128]{0:T(128)S(1)} %copy-done.2), custom_call_target="tpu_custom_call" | custom-call | tf_op jit(solution)/shard_map/pallas_call | solution.py:305
  (2 shorter events, 0.1 us)
Async XLA Ops:
  0.0 1.4 %copy-start.2 = (s32[128]{0:T(128)S(1)}, s32[128]{0:T(128)}, u32[]{:S(2)}) copy-start(s32[128]{0:T(128)} %wave_ref.1) | copy-start | bytes 1540
  0.0 1.5 %copy-start = (bf16[4,4,3,128,128]{4,3,2,1,0:T(8,128)(2,1)S(1)}, bf16[4,4,3,128,128]{4,3,2,1,0:T(8,128)(2,1)}, u32[]{:S(2)}) copy-start(bf16[4,4,3,128,128]{4,3,2,1,0:T(8,128)(2,1)} %w_ref.1) | copy-start | bytes 4718596
  0.0 1.5 %copy-start.4 = (s32[4]{0:T(128)S(1)}, s32[4]{0:T(128)}, u32[]{:S(2)}) copy-start(s32[4]{0:T(128)} %block_ref.1) | copy-start | bytes 52
  0.0 1.5 %copy-start.3 = (s32[4]{0:T(128)S(1)}, s32[4]{0:T(128)}, u32[]{:S(2)}) copy-start(s32[4]{0:T(128)} %row_ref.1) | copy-start | bytes 52
  1.3 14.5 %copy-start.1 = (bf16[32,16,1280]{2,1,0:T(8,128)(2,1)S(1)}, bf16[32,16,1280]{2,1,0:T(8,128)(2,1)}, u32[]{:S(2)}) copy-start(bf16[32,16,1280]{2,1,0:T(8,128)(2,1)} %legendre_ref.1) | copy-start | bytes 3932164

commit v4 on v3

--- a/solution.py
+++ b/solution.py
@@ -49,15 +49,16 @@
             device_id_type=MESH,
         )
 
+    row_order = sorted(range(lat_rows), key=lambda i: -min(i, lat_rows - 1 - i))
     first_row = {1: lat_rows - HALO, -1: 0}
     landing = {1: 0, -1: HALO + lat_rows}
 
-    def lev_copy(n, step):
+    def lev_copy(n, step, i):
         return pltpu.make_async_remote_copy(
-            src_ref=x_ref.at[:, depth - 1 if step > 0 else 0],
-            dst_ref=edges.at[n, pl.ds(HALO, lat_rows)],
-            send_sem=lev_send.at[n],
-            recv_sem=lev_recv.at[n],
+            src_ref=x_ref.at[i, depth - 1 if step > 0 else 0],
+            dst_ref=edges.at[n, HALO + i],
+            send_sem=lev_send.at[n, i],
+            recv_sem=lev_recv.at[n, i],
             device_id={"band": band, "lev": lev + step},
             device_id_type=MESH,
         )
@@ -72,22 +73,26 @@
             device_id_type=MESH,
         )
 
-    def corner_copy(n, m, step):
+    def corner_copy(n, m, step, i):
         return pltpu.make_async_remote_copy(
-            src_ref=edges.at[n, pl.ds(HALO + first_row[step], HALO)],
-            dst_ref=edges.at[n, pl.ds(landing[step], HALO)],
-            send_sem=corner_send.at[n, m],
-            recv_sem=corner_recv.at[n, m],
+            src_ref=edges.at[n, HALO + i],
+            dst_ref=edges.at[n, landing[step] + i - first_row[step]],
+            send_sem=corner_send.at[n, m, i],
+            recv_sem=corner_recv.at[n, m, i],
             device_id={"band": band + step, "lev": lev},
             device_id_type=MESH,
         )
 
+    def corner_rows(step):
+        return range(first_row[step], first_row[step] + HALO)
+
     near_levs = jnp.minimum(lev, 1) + jnp.minimum(levs - 1 - lev, 1)
     pl.semaphore_wait(barrier, bands - 1 + near_levs)
     for n, step in enumerate(SIDES):
         @pl.when(has(lev, step, levs))
         def _(n=n, step=step):
-            lev_copy(n, step).start()
+            for i in row_order:
+                lev_copy(n, step, i).start()
     for n, step in enumerate(SIDES):
         @pl.when(has(band, step, bands))
         def _(n=n, step=step):
@@ -140,14 +145,16 @@
                 jnp.where(base == moved, 1.0, 0.0).astype(picks.dtype)
             )
 
-    for n, step in enumerate(SIDES):
-        @pl.when(has(lev, -step, levs))
-        def _(n=n, step=step):
-            lev_copy(n, step).wait_recv()
-            for m, side in enumerate(SIDES):
-                @pl.when(has(band, side, bands))
-                def _():
-                    corner_copy(n, m, side).start()
+    for i in row_order:
+        for n, step in enumerate(SIDES):
+            @pl.when(has(lev, -step, levs))
+            def _(i=i, n=n, step=step):
+                lev_copy(n, step, i).wait_recv()
+                for m, side in enumerate(SIDES):
+                    if i in corner_rows(side):
+                        @pl.when(has(band, side, bands))
+                        def _():
+                            corner_copy(n, m, side, i).start()
     for n, step in enumerate(SIDES):
         @pl.when(has(band, -step, bands))
         def _(n=n, step=step):
@@ -178,7 +185,8 @@
         for m, side in enumerate(SIDES):
             @pl.when(jnp.logical_and(has(lev, -step, levs), has(band, -side, bands)))
             def _(n=n, m=m, side=side):
-                corner_copy(n, m, side).wait_recv()
+                for i in corner_rows(side):
+                    corner_copy(n, m, side, i).wait_recv()
 
     for r in range(lat_rows):
         start = r + HALO + row_ref[r]
@@ -223,7 +231,8 @@
     for n, step in enumerate(SIDES):
         @pl.when(has(lev, step, levs))
         def _(n=n, step=step):
-            lev_copy(n, step).wait_send()
+            for i in range(lat_rows):
+                lev_copy(n, step, i).wait_send()
 
         @pl.when(has(band, step, bands))
         def _(n=n, step=step):
@@ -231,7 +240,8 @@
             for m in range(2):
                 @pl.when(has(lev, -SIDES[m], levs))
                 def _():
-                    corner_copy(m, n, step).wait_send()
+                    for i in corner_rows(step):
+                        corner_copy(m, n, step, i).wait_send()
     for k in range(1, bands):
         all_copy(k).wait_recv()
         origin = lax.rem(band + bands - k, bands)
@@ -355,12 +365,12 @@
             pltpu.VMEM((lat_rows, blocks, slots, BLK), bf16),
             pltpu.VMEM((bands, lat_rows * slots, BLK), bf16),
             pltpu.VMEM((bands, lat_rows * slots, BLK), bf16),
+            pltpu.SemaphoreType.DMA((2, lat_rows)),
+            pltpu.SemaphoreType.DMA((2, lat_rows)),
             pltpu.SemaphoreType.DMA((2,)),
             pltpu.SemaphoreType.DMA((2,)),
-            pltpu.SemaphoreType.DMA((2,)),
-            pltpu.SemaphoreType.DMA((2,)),
-            pltpu.SemaphoreType.DMA((2, 2)),
-            pltpu.SemaphoreType.DMA((2, 2)),
+            pltpu.SemaphoreType.DMA((2, 2, lat_rows)),
+            pltpu.SemaphoreType.DMA((2, 2, lat_rows)),
             pltpu.SemaphoreType.DMA((bands,)),
             pltpu.SemaphoreType.DMA((bands,)),
         ],

time: 18.6 us -> 18.6 us (level)
  no operation moved by 1% of the time
where the time goes in v4:
time: 18.6 us; the launch traced here: 18.5 us
  Pallas kernels  16.9 us (91%)
  local copies, waits for them, and re-layouts  1.5 us (8%)
    pallas_call x1, Pallas kernels, per_device(): pl.pallas_call(functools.partial(spectral_kernel, bands, levs, fields), o...  14.2 us
    pallas_call x1, Pallas kernels, legendre_tiled(): pl.pallas_call(functools.partial(legendre_kernel, items), out_shape=jax.S...  2.65 us
    reshape x1, local copies, waits for them, and re-layouts, per_device(): x = grid_in.reshape(fields, depth, lat_rows, blocks, BLK)  1.17 us

profile of v4, /device:TPU:9, one launch (start us, length us, event | category | flops | bytes accessed | tf_op | source)
XLA Modules:
  0.0 18.5 jit_solution(18177056111631580321)
XLA Ops:
  0.0 0.0 copy-start.2
  0.0 0.0 copy-start
  0.0 0.0 copy-start.4
  0.0 0.0 copy-start.3
  0.0 1.2 %reshape.12 = bf16[3,4,4,21,128]{4,3,2,1,0:T(8,128)(2,1)S(1)} reshape(bf16[3,4,4,2688]{3,2,1,0:T(4,128)(2,1)} %param.6) | data formatting | bytes 516096 | tf_op jit(solution)/shard_map/reshape | solution.py:349
  1.2 0.1 copy.8
  1.3 0.0 copy-start.1
  1.4 0.0 copy-done.2
  1.5 0.1 copy-done
  1.5 0.0 copy-done.4
  1.6 0.0 copy-done.3
  1.6 14.2 %shard_map.64.coeff_ref = bf16[4,64,128]{2,1,0:T(8,128)(2,1)S(1)} custom-call(bf16[4,4,64,128]{3,2,1,0:T(8,128)(2,1)S(1)} %pad.4.x_ref, bf16[4,4,3,128,128]{4,3,2,1,0:T(8,128)(2,1)S(1)} %copy-done, s32[4]{0:T(128)S(1)} %copy-done.3, s32[4]{0:T(128)S(1)} %copy-done.4, s32[1,128]{1,0:T(1,128)S(1)} %bitcast.4), custom_call_target="tpu_custom_call" | custom-call | tf_op jit(solution)/shard_map/pallas_call | solution.py:354
  15.8 0.0 copy-done.1
  15.8 2.6 %shard_map.65 = bf16[12,32,2,1280]{3,2,1,0:T(2,128)(2,1)} custom-call(bf16[4,64,128]{2,1,0:T(8,128)(2,1)S(1)} %shard_map.64.coeff_ref, bf16[32,16,1280]{2,1,0:T(8,128)(2,1)S(1)} %copy-done.1, s32[128]{0:T(128)S(1)} %copy-done.2), custom_call_target="tpu_custom_call" | custom-call | tf_op jit(solution)/shard_map/pallas_call | solution.py:315
  (2 shorter events, 0.1 us)
Async XLA Ops:
  0.0 1.4 %copy-start.2 = (s32[128]{0:T(128)S(1)}, s32[128]{0:T(128)}, u32[]{:S(2)}) copy-start(s32[128]{0:T(128)} %wave_ref.1) | copy-start | bytes 1540
  0.0 1.5 %copy-start = (bf16[4,4,3,128,128]{4,3,2,1,0:T(8,128)(2,1)S(1)}, bf16[4,4,3,128,128]{4,3,2,1,0:T(8,128)(2,1)}, u32[]{:S(2)}) copy-start(bf16[4,4,3,128,128]{4,3,2,1,0:T(8,128)(2,1)} %w_ref.1) | copy-start | bytes 4718596
  0.0 1.5 %copy-start.4 = (s32[4]{0:T(128)S(1)}, s32[4]{0:T(128)}, u32[]{:S(2)}) copy-start(s32[4]{0:T(128)} %block_ref.1) | copy-start | bytes 52
  0.0 1.5 %copy-start.3 = (s32[4]{0:T(128)S(1)}, s32[4]{0:T(128)}, u32[]{:S(2)}) copy-start(s32[4]{0:T(128)} %row_ref.1) | copy-start | bytes 52
  1.3 14.5 %copy-start.1 = (bf16[32,16,1280]{2,1,0:T(8,128)(2,1)S(1)}, bf16[32,16,1280]{2,1,0:T(8,128)(2,1)}, u32[]{:S(2)}) copy-start(bf16[32,16,1280]{2,1,0:T(8,128)(2,1)} %legendre_ref.1) | copy-start | bytes 3932164
